TPU v7x, 128 devices: a whole 4x4x4 slice. The times are simulated.
128 devices in a mesh: sky: 16 (over z, y), exp: 8 (over x, core).
Axes of the slice: x: 4, y: 4, z: 4, core: 2. Of those that a mesh axis runs over, the one named last changes fastest.
Arguments:
- sky_model: bfloat16 [4096, 1024], P('sky'), may hold values from -6 to 6
- exposure_data: bfloat16 [2048, 128, 128], P(('sky', 'exp')), may hold values from -6 to 6
- pixel_mask: int32 [2048, 128, 128], P(('sky', 'exp')), may hold values 0 or 1
- block_owner: int32 [2048, 1], P(('sky', 'exp')), may hold values from 0 to 15; in each aligned block of 16 rows (0 to 15, 16 to 31, ...) at most 2 rows name the same one
- block_local: int32 [2048], P(('sky', 'exp')), may hold values from 0 to 15
- psf_cell: int32 [2048], P(('sky', 'exp')), may hold values from 0 to 15
- psf_table: bfloat16 [128, 1681], P('exp'), may hold values from -0.15625 to 0.15625
Outputs:
- model_grad: float32 [4096, 1024], P('sky', 'exp')
- residual: bfloat16 [2048, 128, 128], P(('sky', 'exp'))
Inputs may be any that keep to these rules, and one draw needn't show every extreme that they name: `block_owner`: among the pieces of one device no sky index is named more than 2 times.
All inputs are finite; a program needn't handle non-finite values. No bound on the sum of `pixel_mask` on one device may be relied on, other than what follows from the above.
Results may differ from a plain program's by a relative error of at most 0.014.
Values may be sent and summed in bfloat16 or wider, within the bound.
No kernel may reach another device: no remote copies, remote signals or barrier semaphores. Data moves between devices by JAX's collectives and lax.ppermute only.
A program may use at most 64 MiB of HBM per device.

v0:
```python
import jax
import jax.numpy as jnp
from jax import lax
from jax.sharding import PartitionSpec as P

B = 128
PSF = 41
HALO = 20
CAP = 2


def from_behind(x, axis, by):
    devices = lax.axis_size(axis)
    pairs = [(i, i + by) for i in range(devices) if 0 <= i + by < devices]
    return lax.ppermute(x, axis, pairs)


def banded_table(out_cols):
    width = out_cols + PSF - 1
    tap_index = lax.broadcasted_iota(jnp.int32, (PSF, width, out_cols), 0)
    column = lax.broadcasted_iota(jnp.int32, (PSF, width, out_cols), 1)
    target = lax.broadcasted_iota(jnp.int32, (PSF, width, out_cols), 2)
    return (column - target == tap_index).astype(jnp.bfloat16)


def correlate(field, kernel, table, out_rows):
    out_cols = table.shape[2]
    width = field.shape[1]
    banded = jnp.einsum("ab,bcj->caj", kernel, table, preferred_element_type=jnp.float32).astype(
        jnp.bfloat16
    )
    spread = jnp.dot(
        field, banded.reshape(width, PSF * out_cols), preferred_element_type=jnp.float32
    )
    total = spread[0:out_rows, 0:out_cols]
    for offset in range(1, PSF):
        total = (
            total + spread[offset : offset + out_rows, offset * out_cols : (offset + 1) * out_cols]
        )
    return total


def fold_blocks(per_block, block_rows, per_row):
    extent = B + 2 * HALO
    margin = 2 * HALO
    grid = per_block.reshape(block_rows, per_row, extent, extent)
    col_main = grid[..., :B].transpose(0, 2, 1, 3).reshape(block_rows, extent, per_row * B)
    col_tail = jnp.pad(grid[..., B:], ((0, 0), (0, 0), (0, 0), (0, B - margin)))
    col_tail = col_tail.transpose(0, 2, 1, 3).reshape(block_rows, extent, per_row * B)
    width = per_row * B + margin
    columns = (
        jnp.pad(col_main, ((0, 0), (0, 0), (0, margin)))
        + jnp.pad(col_tail, ((0, 0), (0, 0), (B, 0)))[:, :, :width]
    )
    row_main = columns[:, :B].reshape(block_rows * B, width)
    row_tail = jnp.pad(columns[:, B:], ((0, 0), (0, B - margin), (0, 0))).reshape(
        block_rows * B, width
    )
    height = block_rows * B + margin
    return jnp.pad(row_main, ((0, margin), (0, 0))) + jnp.pad(row_tail, ((B, 0), (0, 0)))[:height]


def shards(sky_model, exposure_data, pixel_mask, block_owner, block_local, psf_cell, psf_table):
    sky_count = lax.axis_size("sky")
    extent = B + 2 * HALO
    stripe_rows = sky_model.shape[0]
    stripe_cols = sky_model.shape[1]
    per_row = stripe_cols // B
    block_rows = stripe_rows // B
    block_total = block_rows * per_row
    piece_count = exposure_data.shape[0]
    slot_total = sky_count * CAP
    owner_sky = block_owner[:, 0]
    earlier = lax.broadcasted_iota(jnp.int32, (piece_count, piece_count), 1) < lax.broadcasted_iota(
        jnp.int32, (piece_count, piece_count), 0
    )
    same_owner = owner_sky[:, None] == owner_sky[None, :]
    rank_within = jnp.sum((same_owner & earlier).astype(jnp.int32), axis=1)
    slot_index = owner_sky * CAP + rank_within
    requests = (
        jnp.full((slot_total,), -1, jnp.int32)
        .at[slot_index]
        .set(block_local)
        .reshape(sky_count, CAP)
    )
    cell_count = psf_table.shape[0]
    cell_onehot = (psf_cell[:, None] == lax.broadcasted_iota(jnp.int32, (1, cell_count), 1)).astype(
        jnp.bfloat16
    )
    kernels_flat = jnp.dot(cell_onehot, psf_table, preferred_element_type=jnp.float32).astype(
        jnp.bfloat16
    )
    forward_table = banded_table(B)
    adjoint_table = banded_table(extent)

    def per_piece(item):
        patch, kernel, observed, keep = item
        predicted = correlate(patch, kernel, forward_table, B)
        residual = (keep.astype(jnp.float32) * (predicted - observed.astype(jnp.float32))).astype(
            jnp.bfloat16
        )
        widened = jnp.pad(residual, 2 * HALO)
        adjoint = correlate(widened, kernel[::-1, ::-1], adjoint_table, extent)
        return (residual, adjoint)

    whole = lax.all_gather(sky_model, "sky", axis=0, tiled=True)
    padded = jnp.pad(whole, HALO)
    row_start = (owner_sky * block_rows + block_local // per_row) * B
    col_start = block_local % per_row * B

    def cut_patch(row_first, col_first):
        return lax.dynamic_slice(padded, (row_first, col_first), (extent, extent))

    patches = jax.vmap(cut_patch)(row_start, col_start)
    kernels = kernels_flat.reshape(piece_count, PSF, PSF)
    residuals, adjoints = lax.map(per_piece, (patches, kernels, exposure_data, pixel_mask))
    outgoing = jnp.zeros((slot_total, extent, extent), jnp.float32).at[slot_index].set(adjoints)
    outgoing = outgoing.reshape(sky_count, CAP, extent, extent)
    received, received_ids = (
        lax.all_to_all(
            outgoing.astype(jnp.bfloat16), "sky", split_axis=0, concat_axis=0, tiled=True
        ).astype(outgoing.dtype),
        lax.all_to_all(requests, "sky", split_axis=0, concat_axis=0, tiled=True),
    )
    contributions = received.reshape(slot_total, extent, extent)
    asked_ids = received_ids.reshape(slot_total)
    selector = (asked_ids[:, None] == lax.broadcasted_iota(jnp.int32, (1, block_total), 1)).astype(
        jnp.float32
    )
    per_block = jnp.einsum("nl,nuv->luv", selector, contributions, precision=lax.Precision.HIGHEST)
    canvas = fold_blocks(per_block, block_rows, per_row)
    core = canvas[:, HALO : HALO + stripe_cols]
    from_below = from_behind(core[:HALO].astype(jnp.bfloat16), "sky", -1).astype(jnp.float32)
    from_above = from_behind(core[stripe_rows + HALO :].astype(jnp.bfloat16), "sky", 1).astype(
        jnp.float32
    )
    middle = core[HALO : stripe_rows + HALO]
    folded = (
        middle
        + jnp.pad(from_above, ((0, stripe_rows - HALO), (0, 0)))
        + jnp.pad(from_below, ((stripe_rows - HALO, 0), (0, 0)))
    )
    gradient = lax.psum_scatter(
        folded.astype(jnp.bfloat16), "exp", scatter_dimension=1, tiled=True
    ).astype(jnp.float32)
    return (gradient, residuals)


def solution(mesh):
    in_specs = (
        P("sky", None),
        P(("sky", "exp"), None, None),
        P(("sky", "exp"), None, None),
        P(("sky", "exp"), None),
        P(("sky", "exp")),
        P(("sky", "exp")),
        P("exp", None),
    )
    out_specs = (P("sky", "exp"), P(("sky", "exp"), None, None))
    return jax.shard_map(shards, mesh=mesh, in_specs=in_specs, out_specs=out_specs, check_vma=False)
```

profile of v0, /device:TPU:0, one launch (start us, length us, event | category | flops | bytes accessed | tf_op | source)
XLA Modules:
  0.0 443.7 jit_solution(5079500784704721920)
XLA Ops:
  10.9 8.1 %all-to-all-start = ((s32[16,1,2]{2,1,0:T(1,128)}), s32[16,1,2]{2,1,0:T(1,128)S(1)}, u32[]{:S(2)}, u32[]{:S(2)}) async-start(s32[16,1,2]{2,1,0:T(1,128)} %bitcast.3), calls=%async_computation | async-start | bytes 16384 | tf_op jit(solution)/shard_map/all_to_all | solution.py:123
  20.9 62.6 %all-gather.2.cloned.1.call-done = bf16[4096,1024]{1,0:T(8,128)(2,1)} async-done(((bf16[256,1024]{1,0:T(8,128)(2,1)}), bf16[4096,1024]{1,0:T(8,128)(2,1)}) %all-gather.2.cloned.1.call-update) | async-done | bytes 8388624 | tf_op jit(solution)/shard_map/all_gather | solution.py:106
  83.5 14.8 %pad.49 = bf16[4136,1064]{1,0:T(8,128)(2,1)} pad(bf16[4096,1024]{1,0:T(8,128)(2,1)} %all-gather.2.cloned.1.call-done, bf16[]{:T(256)} %constant.73.clone.1), padding=20_20x20_20 | pad | bytes 17190018 | tf_op jit(solution)/shard_map/jit(_pad)/pad | solution.py:107
  98.3 58.3 %while.16 = (s32[]{:T(128)}, bf16[4136,1064]{1,0:T(8,128)(2,1)}, s32[16,2]{0,1:T(2,128)S(1)}, bf16[16,168,168]{2,1,0:T(8,128)(2,1)}, s32[]{:T(128)}) while((s32[]{:T(128)}, bf16[4136,1064]{1,0:T(8,128)(2,1)}, s32[16,2]{0,1:T(2,128)S(1)}, bf16[16,168,168]{2,1,0:T(8,128)(2,1)}, s32[]{:T(128)}) %tuple.53), condition=%wide.while_cond, body=%wide.while_body.sunk | while | flops 2 | bytes 173665 | solution.py:112
  99.0 3.0 bitcast_dynamic-update-slice_fusion.4
  102.6 3.0 bitcast_dynamic-update-slice_fusion.4
  106.3 3.0 bitcast_dynamic-update-slice_fusion.4
  113.5 3.0 bitcast_dynamic-update-slice_fusion.4
  117.2 3.0 bitcast_dynamic-update-slice_fusion.4
  128.1 3.0 bitcast_dynamic-update-slice_fusion.4
  131.8 3.0 bitcast_dynamic-update-slice_fusion.4
  135.4 3.0 bitcast_dynamic-update-slice_fusion.4
  139.1 3.0 bitcast_dynamic-update-slice_fusion.4
  142.7 3.0 bitcast_dynamic-update-slice_fusion.4
  146.4 3.0 bitcast_dynamic-update-slice_fusion.4
  156.6 157.8 %while.17 = (s32[]{:T(128)}, bf16[16,128,128]{2,1,0:T(8,128)(2,1)}, f32[16,168,168]{2,1,0:T(8,128)S(1)}, s32[16,128,128]{2,1,0:T(8,128)}, bf16[16,168,168]{2,1,0...) while((s32[]{:T(128)}, bf16[16,128,128]{2,1,0:T(8,128)(2,1)}, ...), condition=%wide.region_3.4_spmd.clone, body=%wide.region_2.3_spmd.clone.sunk | while | flops 1093145856 | bytes 34470920 | solution.py:116
  317.2 4.1 scatter_fusion
  324.2 3.7 copy.17
  327.9 5.2 %all-to-all-start.1 = ((bf16[16,2,168,168]{3,1,2,0:T(2,128)(2,1)}), bf16[16,2,168,168]{3,1,2,0:T(2,128)(2,1)S(1)}, u32[]{:S(2)}, u32[]{:S(2)}) async-start(bf16[16,2,168,168]{3,1,2,0:T(2,128)(2,1)} %copy.17), calls=%async_computation.1 | async-start | bytes 5505024 | tf_op jit(solution)/shard_map/all_to_all | solution.py:120
  334.7 40.4 %all-to-all-done.1 = bf16[16,2,168,168]{3,1,2,0:T(2,128)(2,1)S(1)} async-done(((bf16[16,2,168,168]{3,1,2,0:T(2,128)(2,1)}), bf16[16,2,168,168]{3,1,2,0:T(2,128)(2,1)S(1)}, u32[]{:S(2)}, u32[]{:S(2)}) %all-to-all-start.1) | async-done | bytes 1806368 | tf_op jit(solution)/shard_map/all_to_all | solution.py:120
  375.1 4.7 %copy.18 = bf16[16,2,168,168]{3,1,0,2:T(2,128)(2,1)} copy(bf16[16,2,168,168]{3,1,2,0:T(2,128)(2,1)S(1)} %all-to-all-done.1) | data formatting | bytes 3612672 | tf_op jit(solution)/shard_map/all_to_all | solution.py:120
  379.8 5.7 %reshape.115 = bf16[32,168,168,1]{2,0,1,3:T(8,128)(2,1)S(1)} reshape(bf16[16,2,168,168]{3,1,0,2:T(2,128)(2,1)} %copy.18) | data formatting | bytes 3612672 | tf_op jit(solution)/shard_map/reshape | solution.py:125
  395.3 4.3 collective-permute-done.1
  400.9 34.3 %reduce-scatter.4.cloned.1.call-done = bf16[128,256]{1,0:T(8,128)(2,1)} async-done(((bf16[1024,256]{1,0:T(8,128)(2,1)}), bf16[128,256]{1,0:T(8,128)(2,1)}) %reduce-scatter.4.cloned.1.call-update) | async-done | bytes 65552
  (226 shorter events, 207.9 us)
Async XLA Ops:
  7.2 11.9 %copy-start = (bf16[16,1681]{1,0:T(8,128)(2,1)S(1)}, bf16[16,1681]{1,0:T(8,128)(2,1)}, u32[]{:S(2)}) copy-start(bf16[16,1681]{1,0:T(8,128)(2,1)} %param.15) | copy-start | bytes 161380
  7.2 76.3 %all-gather.2.cloned.1.call-start = ((), (), s32[]{:S(2)}) async-start(), calls=%async_computation.3 | async-start | bytes 8912896 | tf_op jit(solution)/shard_map/all_gather | solution.py:106
  10.9 316.9 %all-to-all-start = ((s32[16,1,2]{2,1,0:T(1,128)}), s32[16,1,2]{2,1,0:T(1,128)S(1)}, u32[]{:S(2)}, u32[]{:S(2)}) async-start(s32[16,1,2]{2,1,0:T(1,128)} %bitcast.3), calls=%async_computation | async-start | bytes 16384 | tf_op jit(solution)/shard_map/all_to_all | solution.py:123
  327.9 47.2 %all-to-all-start.1 = ((bf16[16,2,168,168]{3,1,2,0:T(2,128)(2,1)}), bf16[16,2,168,168]{3,1,2,0:T(2,128)(2,1)S(1)}, u32[]{:S(2)}, u32[]{:S(2)}) async-start(bf16[16,2,168,168]{3,1,2,0:T(2,128)(2,1)} %copy.17), calls=%async_computation.1 | async-start | bytes 5505024 | tf_op jit(solution)/shard_map/all_to_all | solution.py:120
  333.1 102.1 %reduce-scatter.4.cloned.1.call-start = ((), (), s32[]{:S(2)}) async-start(), calls=%async_computation.4 | async-start | bytes 589824
  392.0 44.8 %copy-start.1 = (bf16[16,1681]{1,0:T(8,128)(2,1)S(1)}, bf16[16,1681]{1,0:T(8,128)(2,1)}, u32[]{:S(2)}) copy-start(bf16[16,1681]{1,0:T(8,128)(2,1)} %param.15) | copy-start | bytes 161380
  392.3 3.0 collective-permute-start
  393.6 6.0 %collective-permute-start.1 = (bf16[20,1024]{1,0:T(8,128)(2,1)S(1)}, bf16[20,1024]{1,0:T(8,128)(2,1)S(1)}, u32[]{:S(2)}, u32[]{:S(2)}) collective-permute-start(bf16[20,1024]{1,0:T(8,128)(2,1)S(1)} %get-tuple-element.172), channel_id=1, source_target_pairs={{8,0},{16,8},{24,16},{32,24},{40,32},{48,40},{56,48},{64,56},{72,6... | collective-permute-start | bytes 122888 | tf_op jit(solution)/shard_map/ppermute | solution.py:15
Sparse Core Ops, SparseCore 0:
  10.2 73.3 all-gather.1
  401.0 34.1 reduce-scatter.3
where the time goes:
time: 446 us; the launch traced here: 444 us
  waiting for transfers between devices  143 us (32%)
  local copies, waits for them, and re-layouts  125 us (28%)
  matrix products  77.6 us (17%)
  other arithmetic  67.5 us (15%)
  starting transfers between devices  16.3 us (4%)
  between operations  14.3 us (3%)
    all_gather x1, waiting for transfers between devices, shards(): whole = lax.all_gather(sky_model, 'sky', axis=0, tiled=True)  62.6 us
    dynamic_update_slice x32, other arithmetic, shards(): lax.map(per_piece, (patches, kernels, exposure_data, pixel_mask))  59 us
    gather x48, local copies, waits for them, and re-layouts  58.3 us
    dot_general x32, matrix products, correlate(): jnp.dot(field, banded.reshape(width, PSF * out_cols), preferred_element_t...  45.9 us
    all_to_all x1, waiting for transfers between devices, shards(): lax.all_to_all(outgoing.astype(jnp.bfloat16), 'sky', split_axis=0, concat...  40.4 us
    unnamed x3, waiting for transfers between devices  35 us
    dot_general x32, matrix products, correlate(): jnp.einsum('ab,bcj->caj', kernel, table, preferred_element_type=jnp.float32)  30.2 us
    convert_element_type x16, local copies, waits for them, and re-layouts, correlate(): jnp.einsum('ab,bcj->caj', kernel, table, preferred_element_type=jnp.float32)  20.1 us
  transfers between devices with their start and end apart: 6, of which 5 were waited for; matrix products, arithmetic and copies ran while one was open for 56% of the time, Pallas kernels for 0%

commit v1 on v0

--- a/solution.py
+++ b/solution.py
@@ -103,7 +103,9 @@
         adjoint = correlate(widened, kernel[::-1, ::-1], adjoint_table, extent)
         return (residual, adjoint)
 
-    whole = lax.all_gather(sky_model, "sky", axis=0, tiled=True)
+    whole = jnp.concatenate(
+        lax.all_to_all(jnp.stack([sky_model] * lax.axis_size("sky")), "sky", 0, 0), axis=0
+    )
     padded = jnp.pad(whole, HALO)
     row_start = (owner_sky * block_rows + block_local // per_row) * B
     col_start = block_local % per_row * B

time: 446 us -> 508 us (1.14)
  waiting for transfers between devices: 143 us -> 197 us
  starting transfers between devices: 16.3 us -> 24 us
    all_to_all x0 -> x1, waiting for transfers between devices: none -> 122 us  [shards(): lax.all_to_all(jnp.stack([sky_model] * lax.axis_size('sky')), 'sky', 0, 0)]
    all_gather x1 -> x0, waiting for transfers between devices: 62.6 us -> none  [shards(): whole = lax.all_gather(sky_model, 'sky', axis=0, tiled=True)]
    all_to_all x0 -> x1, starting transfers between devices: none -> 8.31 us  [shards(): lax.all_to_all(jnp.stack([sky_model] * lax.axis_size('sky')), 'sky', 0, 0)]
    another operation x0 -> x1, local copies, waits for them, and re-layouts: none -> 5.36 us  [shards(): jnp.stack([sky_model] * lax.axis_size('sky'))]
    unnamed x3 -> x2, waiting for transfers between devices: 35 us -> 34.6 us
  transfers between devices with their start and end apart: 6 -> 6, of which waited for: 5 -> 5; matrix products, arithmetic and copies ran while one was open for 56% -> 48% of each run, Pallas kernels for 0% -> 0%
where the time goes in v1:
time: 508 us; the launch traced here: 505 us
  waiting for transfers between devices  197 us (39%)
  local copies, waits for them, and re-layouts  127 us (25%)
  matrix products  76.9 us (15%)
  other arithmetic  65.4 us (13%)
  starting transfers between devices  24 us (5%)
  between operations  14.3 us (3%)
    all_to_all x1, waiting for transfers between devices, shards(): lax.all_to_all(jnp.stack([sky_model] * lax.axis_size('sky')), 'sky', 0, 0)  122 us
    dynamic_update_slice x32, other arithmetic, shards(): lax.map(per_piece, (patches, kernels, exposure_data, pixel_mask))  59 us
    gather x48, local copies, waits for them, and re-layouts  55.3 us
    dot_general x32, matrix products, correlate(): jnp.dot(field, banded.reshape(width, PSF * out_cols), preferred_element_t...  45.9 us
    all_to_all x1, waiting for transfers between devices, shards(): lax.all_to_all(outgoing.astype(jnp.bfloat16), 'sky', split_axis=0, concat...  35.6 us
    unnamed x2, waiting for transfers between devices  34.6 us
    dot_general x32, matrix products, correlate(): jnp.einsum('ab,bcj->caj', kernel, table, preferred_element_type=jnp.float32)  30.2 us
    convert_element_type x16, local copies, waits for them, and re-layouts, correlate(): jnp.einsum('ab,bcj->caj', kernel, table, preferred_element_type=jnp.float32)  20.1 us
  transfers between devices with their start and end apart: 6, of which 5 were waited for; matrix products, arithmetic and copies ran while one was open for 48% of the time, Pallas kernels for 0%

profile of v1, /device:TPU:0, one launch (start us, length us, event | category | flops | bytes accessed | tf_op | source)
XLA Modules:
  0.0 505.1 jit_solution(705098838889908942)
XLA Ops:
  7.2 5.4 %stack.2 = bf16[16,256,1024]{2,1,0:T(8,128)(2,1)} broadcast(bf16[256,1024]{1,0:T(8,128)(2,1)} %param.9), dimensions={1,2} | broadcast | bytes 8912896 | tf_op jit(solution)/shard_map/stack | solution.py:107
  12.5 8.3 %all-to-all-start.1 = ((bf16[16,256,1024]{2,1,0:T(8,128)(2,1)}), bf16[16,256,1024]{2,1,0:T(8,128)(2,1)}, u32[]{:S(2)}, u32[]{:S(2)}) async-start(bf16[16,256,1024]{2,1,0:T(8,128)(2,1)} %stack.2), calls=%async_computation.1 | async-start | bytes 16777216 | tf_op jit(solution)/shard_map/all_to_all | solution.py:107
  22.9 122.0 %all-to-all-done.1 = bf16[16,256,1024]{2,1,0:T(8,128)(2,1)} async-done(((bf16[16,256,1024]{2,1,0:T(8,128)(2,1)}), bf16[16,256,1024]{2,1,0:T(8,128)(2,1)}, u32[]{:S(2)}, u32[]{:S(2)}) %all-to-all-start.1) | async-done | bytes 8388640 | tf_op jit(solution)/shard_map/all_to_all | solution.py:107
  144.9 5.7 %all-to-all-start = ((s32[16,1,2]{2,1,0:T(1,128)}), s32[16,1,2]{2,1,0:T(1,128)S(1)}, u32[]{:S(2)}, u32[]{:S(2)}) async-start(s32[16,1,2]{2,1,0:T(1,128)} %bitcast.3), calls=%async_computation | async-start | bytes 16384 | tf_op jit(solution)/shard_map/all_to_all | solution.py:125
  150.6 14.8 %pad.49 = bf16[4136,1064]{1,0:T(8,128)(2,1)} pad(bf16[4096,1024]{1,0:T(8,128)(2,1)} %bitcast.6, bf16[]{:T(256)} %constant.73.clone.1), padding=20_20x20_20 | pad | bytes 17190018 | tf_op jit(solution)/shard_map/jit(_pad)/pad | solution.py:109
  165.3 55.4 %while.16 = (s32[]{:T(128)}, bf16[4136,1064]{1,0:T(8,128)(2,1)}, s32[16,2]{0,1:T(2,128)S(1)}, bf16[16,168,168]{2,1,0:T(8,128)(2,1)}, s32[]{:T(128)}) while((s32[]{:T(128)}, bf16[4136,1064]{1,0:T(8,128)(2,1)}, s32[16,2]{0,1:T(2,128)S(1)}, bf16[16,168,168]{2,1,0:T(8,128)(2,1)}, s32[]{:T(128)}) %tuple.53), condition=%wide.while_cond, body=%wide.while_body.sunk | while | flops 2 | bytes 173665 | solution.py:114
  166.0 2.8 bitcast_dynamic-update-slice_fusion.4
  169.4 2.8 bitcast_dynamic-update-slice_fusion.4
  172.9 2.8 bitcast_dynamic-update-slice_fusion.4
  179.8 2.8 bitcast_dynamic-update-slice_fusion.4
  193.6 2.8 bitcast_dynamic-update-slice_fusion.4
  204.0 2.8 bitcast_dynamic-update-slice_fusion.4
  210.9 2.8 bitcast_dynamic-update-slice_fusion.4
  220.7 157.8 %while.17 = (s32[]{:T(128)}, bf16[16,128,128]{2,1,0:T(8,128)(2,1)}, f32[16,168,168]{2,1,0:T(8,128)S(1)}, s32[16,128,128]{2,1,0:T(8,128)}, bf16[16,168,168]{2,1,0...) while((s32[]{:T(128)}, bf16[16,128,128]{2,1,0:T(8,128)(2,1)}, ...), condition=%wide.region_3.4_spmd.clone, body=%wide.region_2.3_spmd.clone.sunk | while | flops 1093145856 | bytes 34470920 | solution.py:118
  378.4 2.8 broadcast_in_dim.36
  381.3 4.1 scatter_fusion
  385.4 2.8 convert_element_type.99
  388.3 3.7 copy.17
  391.9 7.2 %all-to-all-start.2 = ((bf16[16,2,168,168]{3,1,2,0:T(2,128)(2,1)}), bf16[16,2,168,168]{3,1,2,0:T(2,128)(2,1)S(1)}, u32[]{:S(2)}, u32[]{:S(2)}) async-start(bf16[16,2,168,168]{3,1,2,0:T(2,128)(2,1)} %copy.17), calls=%async_computation.2 | async-start | bytes 5505024 | tf_op jit(solution)/shard_map/all_to_all | solution.py:122
  400.7 35.6 %all-to-all-done.2 = bf16[16,2,168,168]{3,1,2,0:T(2,128)(2,1)S(1)} async-done(((bf16[16,2,168,168]{3,1,2,0:T(2,128)(2,1)}), bf16[16,2,168,168]{3,1,2,0:T(2,128)(2,1)S(1)}, u32[]{:S(2)}, u32[]{:S(2)}) %all-to-all-start.2) | async-done | bytes 1806368 | tf_op jit(solution)/shard_map/all_to_all | solution.py:122
  436.2 4.7 copy.18
  440.9 5.7 %reshape.121 = bf16[32,168,168,1]{2,0,1,3:T(8,128)(2,1)S(1)} reshape(bf16[16,2,168,168]{3,1,0,2:T(2,128)(2,1)} %copy.18) | data formatting | bytes 3612672 | tf_op jit(solution)/shard_map/reshape | solution.py:127
  456.5 4.3 collective-permute-done.1
  462.0 34.6 %reduce-scatter.4.cloned.1.call-done = bf16[128,256]{1,0:T(8,128)(2,1)} async-done(((bf16[1024,256]{1,0:T(8,128)(2,1)}), bf16[128,256]{1,0:T(8,128)(2,1)}) %reduce-scatter.4.cloned.1.call-update) | async-done | bytes 65552
  (232 shorter events, 208.8 us)
Async XLA Ops:
  7.2 13.7 %copy-start = (bf16[16,1681]{1,0:T(8,128)(2,1)S(1)}, bf16[16,1681]{1,0:T(8,128)(2,1)}, u32[]{:S(2)}) copy-start(bf16[16,1681]{1,0:T(8,128)(2,1)} %param.15) | copy-start | bytes 161380
  12.5 8.4 %copy-start.2 = (s32[16]{0:T(128)S(1)}, s32[16]{0:T(128)}, u32[]{:S(2)}) copy-start(s32[16]{0:T(128)} %param.14) | copy-start | bytes 196
  12.5 8.8 %copy-start.3 = (s32[16,1]{0,1:T(1,128)S(1)}, s32[16,1]{0,1:T(1,128)}, u32[]{:S(2)}) copy-start(s32[16,1]{0,1:T(1,128)} %param.12) | copy-start | bytes 196
  12.5 9.0 %copy-start.4 = (s32[16]{0:T(128)S(1)}, s32[16]{0:T(128)}, u32[]{:S(2)}) copy-start(s32[16]{0:T(128)} %param.13) | copy-start | bytes 196
  12.5 132.3 %all-to-all-start.1 = ((bf16[16,256,1024]{2,1,0:T(8,128)(2,1)}), bf16[16,256,1024]{2,1,0:T(8,128)(2,1)}, u32[]{:S(2)}, u32[]{:S(2)}) async-start(bf16[16,256,1024]{2,1,0:T(8,128)(2,1)} %stack.2), calls=%async_computation.1 | async-start | bytes 16777216 | tf_op jit(solution)/shard_map/all_to_all | solution.py:107
  144.9 247.0 %all-to-all-start = ((s32[16,1,2]{2,1,0:T(1,128)}), s32[16,1,2]{2,1,0:T(1,128)S(1)}, u32[]{:S(2)}, u32[]{:S(2)}) async-start(s32[16,1,2]{2,1,0:T(1,128)} %bitcast.3), calls=%async_computation | async-start | bytes 16384 | tf_op jit(solution)/shard_map/all_to_all | solution.py:125
  391.9 44.3 %all-to-all-start.2 = ((bf16[16,2,168,168]{3,1,2,0:T(2,128)(2,1)}), bf16[16,2,168,168]{3,1,2,0:T(2,128)(2,1)S(1)}, u32[]{:S(2)}, u32[]{:S(2)}) async-start(bf16[16,2,168,168]{3,1,2,0:T(2,128)(2,1)} %copy.17), calls=%async_computation.2 | async-start | bytes 5505024 | tf_op jit(solution)/shard_map/all_to_all | solution.py:122
  399.1 97.5 %reduce-scatter.4.cloned.1.call-start = ((), (), s32[]{:S(2)}) async-start(), calls=%async_computation.4 | async-start | bytes 589824
  453.2 45.0 %copy-start.1 = (bf16[16,1681]{1,0:T(8,128)(2,1)S(1)}, bf16[16,1681]{1,0:T(8,128)(2,1)}, u32[]{:S(2)}) copy-start(bf16[16,1681]{1,0:T(8,128)(2,1)} %param.15) | copy-start | bytes 161380
  453.5 3.0 collective-permute-start
  454.8 6.0 %collective-permute-start.1 = (bf16[20,1024]{1,0:T(8,128)(2,1)S(1)}, bf16[20,1024]{1,0:T(8,128)(2,1)S(1)}, u32[]{:S(2)}, u32[]{:S(2)}) collective-permute-start(bf16[20,1024]{1,0:T(8,128)(2,1)S(1)} %get-tuple-element.172), channel_id=1, source_target_pairs={{8,0},{16,8},{24,16},{32,24},{40,32},{48,40},{56,48},{64,56},{72,6... | collective-permute-start | bytes 122888 | tf_op jit(solution)/shard_map/ppermute | solution.py:15
Sparse Core Ops, SparseCore 0:
  462.2 34.3 reduce-scatter.3
